TPU v7x, 32 devices: a whole 2x2x4 slice. The times are simulated.
32 devices in a mesh: groups: 2 (over y), shard: 4 (over z), sub: 2 (over x), chan: 2 (over core).
Axes of the slice: x: 2, y: 2, z: 4, core: 2. Of those that a mesh axis runs over, the one named last changes fastest.
Arguments:
- field: bfloat16 [32, 8, 96, 128], P(('groups', 'shard'), 'sub', 'chan'), parts along dimension 0, may hold values from -6 to 6
- cotangent: bfloat16 [32, 8, 96, 128], P(('groups', 'shard'), 'sub', 'chan'), parts along dimension 0, may hold values from -6 to 6
- space_weight: bfloat16 [3, 3, 96, 96], replicated, may hold values from -0.21875 to 0.21875
- time_weight: bfloat16 [9, 96], P(None, 'chan'), may hold values from -2 to 2
Outputs:
- output: bfloat16 [32, 8, 96, 128], P(('groups', 'shard'), 'sub', 'chan'), parts along dimension 0
- field_grad: bfloat16 [32, 8, 96, 128], P(('groups', 'shard'), 'sub', 'chan'), parts along dimension 0
- space_grad: float32 [6, 3, 96, 96], P('groups', None, 'chan'), parts along dimension 0
- time_grad: float32 [18, 96], P('groups', 'chan'), parts along dimension 0
There are 2 independent parts, one for each index of `groups`. A program takes and returns all parts, laid end to end along the dimension named above; an argument that names none is the same for every part. Nothing has to cross between parts.
All inputs are finite; a program needn't handle non-finite values.
Results may differ from a plain program's by a relative error of at most 0.0048.
Values may be sent and summed in bfloat16 or wider, within the bound.
A program may use at most 64 MiB of HBM per device.

v0:
```python
import jax
import jax.numpy as jnp
from jax import lax
from jax.sharding import PartitionSpec as P


def with_halo(cells, sides, width):
    for axis, dim in sides:
        count = lax.axis_size(axis)
        ends = count - 1
        head = lax.slice_in_dim(cells, 0, width, axis=dim)
        tail = lax.slice_in_dim(cells, cells.shape[dim] - width, cells.shape[dim], axis=dim)
        cells = jnp.concatenate(
            [
                lax.ppermute(tail, axis, [(i, (i + 1) % count) for i in range(ends)]),
                cells,
                lax.ppermute(head, axis, [((i + 1) % count, i) for i in range(ends)]),
            ],
            axis=dim,
        )
    return cells


def gelu_tanh(values):
    return jax.nn.gelu(values, approximate=True)


def widen(values):
    rimmed = with_halo(values, (("sub", 1),), 1)
    gathered = lax.all_gather(rimmed, "chan", axis=2, tiled=True)
    return jnp.pad(gathered, ((0, 0), (0, 0), (0, 0), (1, 1)))


def to_time(values):
    return lax.all_to_all(values, "shard", split_axis=1, concat_axis=0, tiled=True)


def to_space(values):
    return lax.all_to_all(values, "shard", split_axis=0, concat_axis=1, tiled=True)


def pad_time(values):
    return jnp.pad(values, ((4, 4), (0, 0), (0, 0), (0, 0)))


def time_forward(padded, taps, count):
    total = jnp.zeros((count,) + padded.shape[1:], jnp.float32)
    for k in range(9):
        total = total + taps[k][:, None] * padded[k : k + count]
    return total


def time_back(padded, taps, count):
    total = jnp.zeros((count,) + padded.shape[1:], jnp.float32)
    for k in range(9):
        total = total + taps[k][:, None] * padded[8 - k : 8 - k + count]
    return total


def time_weight_part(grads, padded, count):
    grads32 = grads.astype(jnp.float32)
    parts = []
    for k in range(9):
        parts.append(jnp.sum(grads32 * padded[k : k + count], axis=(0, 1, 3)))
    return jnp.stack(parts)


def on_device(field, cotangent, space_weight, time_weight):
    frames_here, rows, width_own, cells = field.shape
    start = lax.axis_index("chan") * width_own
    tap_rows = lax.dynamic_slice_in_dim(space_weight, start, width_own, 2)
    tap_cols = lax.dynamic_slice_in_dim(space_weight, start, width_own, 3)
    taps = time_weight.astype(jnp.float32)
    full = widen(field)
    hidden = jnp.zeros(field.shape, jnp.float32)
    for i in range(3):
        for j in range(3):
            hidden = hidden + jnp.einsum(
                "oc,frcw->frow",
                tap_rows[i, j],
                full[:, i : i + rows, :, j : j + cells],
                preferred_element_type=jnp.float32,
            )
    act, pull = jax.vjp(gelu_tanh, hidden)
    acts = act.astype(jnp.bfloat16)
    acts_time = to_time(acts)
    acts_pad = pad_time(acts_time)
    frames = acts_time.shape[0]
    mixed = to_space(time_forward(acts_pad, taps, frames).astype(jnp.bfloat16))
    grad_time = to_time(cotangent)
    back_local = time_back(pad_time(grad_time), taps, frames).astype(jnp.bfloat16)
    time_part = time_weight_part(grad_time, acts_pad, frames)
    back_time = to_space(back_local)
    output = (field.astype(jnp.float32) + mixed.astype(jnp.float32)).astype(jnp.bfloat16)
    back_hidden = pull(back_time.astype(jnp.float32))[0].astype(jnp.bfloat16)
    wide_grad = widen(back_hidden)
    back_field = cotangent.astype(jnp.float32)
    space_rows = []
    for i in range(3):
        inner = []
        for j in range(3):
            back_field = back_field + jnp.einsum(
                "oc,frow->frcw",
                tap_cols[i, j],
                wide_grad[:, 2 - i : 2 - i + rows, :, 2 - j : 2 - j + cells],
                preferred_element_type=jnp.float32,
            )
            inner.append(
                jnp.einsum(
                    "frow,frcw->oc",
                    back_hidden,
                    full[:, i : i + rows, :, j : j + cells],
                    preferred_element_type=jnp.float32,
                )
            )
        space_rows.append(jnp.stack(inner))
    field_grad = back_field.astype(jnp.bfloat16)
    space_part = jnp.stack(space_rows)
    space_total, time_total = lax.psum((space_part, time_part), ("shard", "sub"))
    total_frames = frames_here * lax.axis_size("shard")
    total_rows = rows * lax.axis_size("sub")
    scale = float(total_frames * total_rows * cells) ** (-0.5)
    return (output, field_grad, space_total * scale, time_total * scale)


def solution(mesh):
    placed = (
        P(("groups", "shard"), "sub", "chan", None),
        P(("groups", "shard"), "sub", "chan", None),
        P(),
        P(None, "chan"),
    )
    return jax.shard_map(
        on_device,
        mesh=mesh,
        in_specs=placed,
        out_specs=(
            P(("groups", "shard"), "sub", "chan", None),
            P(("groups", "shard"), "sub", "chan", None),
            P("groups", None, "chan", None),
            P("groups", "chan"),
        ),
        check_vma=False,
    )
```

profile of v0, /device:TPU:0, one launch (start us, length us, event | category | flops | bytes accessed | tf_op | source)
XLA Modules:
  0.0 162.7 jit_solution(8335515254754302777)
XLA Ops:
  7.2 0.9 fusion.95
  8.1 4.9 %collective-permute-start = (bf16[4,1,48,128]{3,2,1,0:T(8,128)(2,1)S(1)}, bf16[4,1,48,128]{3,2,1,0:T(8,128)(2,1)S(1)}, u32[]{:S(2)}, u32[]{:S(2)}) collective-permute-start(bf16[4,1,48,128]{3,2,1,0:T(8,128)(2,1)S(1)} %get-tuple-element.24), channel_id=1, source_target_pairs={{0,2},{1,3},{4,6},{5,7},{8,10},{9,11},{12,14},{13,15},{16,18},{17,... | collective-permute-start | bytes 147464 | tf_op jit(solution)/shard_map/ppermute | solution.py:15
  13.0 1.3 collective-permute-start.1
  14.3 1.6 copy.19
  15.9 4.9 %all-to-all-start.2 = ((bf16[4,4,48,128]{3,2,0,1:T(8,128)(2,1)}), bf16[4,4,48,128]{3,2,0,1:T(8,128)(2,1)S(1)}, u32[]{:S(2)}, u32[]{:S(2)}) async-start(bf16[4,4,48,128]{3,2,0,1:T(8,128)(2,1)} %copy.19), calls=%async_computation.2 | async-start | bytes 393216 | tf_op jit(solution)/shard_map/all_to_all | solution.py:35
  20.9 2.2 %all_gather.6 = bf16[4,6,96,128]{3,2,1,0:T(8,128)(2,1)S(1)} all-gather(bf16[4,6,48,128]{3,2,1,0:T(8,128)(2,1)S(1)} %pad_maximum_fusion), channel_id=1, replica_groups=mesh['groups'=2,'shard'=4,'sub'=2,'chan'=2] {'chan'}, dimensions={2}, use_global_device_ids=true | all-gather | bytes 884736 | tf_op jit(solution)/shard_map/all_gather | solution.py:30
  23.1 0.3 fusion.55
  23.6 0.3 convolution_add_fusion.6
  23.9 0.3 convolution_add_fusion.5
  24.5 0.3 convolution_add_fusion.3
  24.8 3.2 %all-to-all-done.2 = bf16[4,4,48,128]{3,2,0,1:T(8,128)(2,1)S(1)} async-done(((bf16[4,4,48,128]{3,2,0,1:T(8,128)(2,1)}), bf16[4,4,48,128]{3,2,0,1:T(8,128)(2,1)S(1)}, u32[]{:S(2)}, u32[]{:S(2)}) %all-to-all-start.2) | async-done | bytes 196640 | tf_op jit(solution)/shard_map/all_to_all | solution.py:35
  28.1 1.0 fusion.56
  29.1 3.4 %all-to-all-start.3 = ((bf16[16,1,48,128]{3,2,1,0:T(8,128)(2,1)}), bf16[16,1,48,128]{3,2,1,0:T(8,128)(2,1)S(1)}, u32[]{:S(2)}, u32[]{:S(2)}) async-start(bf16[16,1,48,128]{3,2,1,0:T(8,128)(2,1)} %fusion.56), calls=%async_computation.3 | async-start | bytes 393216 | tf_op jit(solution)/shard_map/all_to_all | solution.py:39
  32.4 0.3 convolution_add_fusion.2
  33.0 5.7 %all-to-all-done.3 = bf16[16,1,48,128]{3,2,1,0:T(8,128)(2,1)S(1)} async-done(((bf16[16,1,48,128]{3,2,1,0:T(8,128)(2,1)}), bf16[16,1,48,128]{3,2,1,0:T(8,128)(2,1)S(1)}, u32[]{:S(2)}, u32[]{:S(2)}) %all-to-all-start.3) | async-done | bytes 196640 | tf_op jit(solution)/shard_map/all_to_all | solution.py:39
  38.7 0.6 fusion.26
  39.5 0.3 convolution_bitcast_fusion.11
  39.8 0.3 convolution_bitcast_fusion.12
  40.1 0.2 convolution_bitcast_fusion.13
  40.4 0.3 convolution_bitcast_fusion.14
  40.7 0.3 convolution_bitcast_fusion.15
  41.1 0.2 convolution_bitcast_fusion.16
  41.3 0.3 convolution_bitcast_fusion.17
  41.7 0.3 convolution_bitcast_fusion.9
  42.0 0.7 copy.16
  42.7 3.4 %all-to-all-start = ((bf16[4,4,48,128]{3,2,0,1:T(8,128)(2,1)}), bf16[4,4,48,128]{3,2,0,1:T(8,128)(2,1)S(1)}, u32[]{:S(2)}, u32[]{:S(2)}) async-start(bf16[4,4,48,128]{3,2,0,1:T(8,128)(2,1)} %copy.16), calls=%async_computation | async-start | bytes 393216 | tf_op jit(solution)/shard_map/all_to_all | solution.py:35
  46.1 4.5 %collective-permute-start.2 = (bf16[4,1,48,128]{3,2,1,0:T(8,128)(2,1)S(1)}, bf16[4,1,48,128]{3,2,1,0:T(8,128)(2,1)S(1)}, u32[]{:S(2)}, u32[]{:S(2)}) collective-permute-start(bf16[4,1,48,128]{3,2,1,0:T(8,128)(2,1)S(1)} %get-tuple-element.22), channel_id=1, source_target_pairs={{0,2},{1,3},{4,6},{5,7},{8,10},{9,11},{12,14},{13,15},{16,18},{17,... | collective-permute-start | bytes 147464 | tf_op jit(solution)/shard_map/ppermute | solution.py:15
  50.7 1.3 collective-permute-start.3
  52.0 0.7 pad_maximum_fusion.2
  52.8 3.9 %collective-permute-done.3 = bf16[4,1,48,128]{3,2,1,0:T(8,128)(2,1)S(1)} collective-permute-done((bf16[4,1,48,128]{3,2,1,0:T(8,128)(2,1)S(1)}, bf16[4,1,48,128]{3,2,1,0:T(8,128)(2,1)S(1)}, u32[]{:S(2)}, u32[]{:S(2)}) %collective-permute-start.3) | collective-permute-done | bytes 49184 | tf_op jit(solution)/shard_map/ppermute | solution.py:17
  56.7 2.4 %all_gather.7 = bf16[4,6,96,128]{3,2,1,0:T(8,128)(2,1)S(1)} all-gather(bf16[4,6,48,128]{3,2,1,0:T(8,128)(2,1)S(1)} %pad_maximum_fusion.1), channel_id=1, replica_groups=mesh['groups'=2,'shard'=4,'sub'=2,'chan'=2] {'chan'}, dimensions={2}, use_global_device_ids=true | all-gather | bytes 884736 | tf_op jit(solution)/shard_map/all_gather | solution.py:30
  59.1 0.3 fusion.8
  59.4 0.3 fusion.7
  59.7 0.3 fusion.6
  60.1 0.3 fusion.5
  60.4 0.3 fusion.4
  60.8 0.3 fusion.3
  61.1 0.3 fusion.2
  61.5 0.3 fusion.1
  61.8 1.0 fusion.10
  62.8 63.5 %all-reduce.6.cloned.1.call-done = f32[3,3,48,96]{3,2,1,0:T(8,128)} async-done(((f32[3,3,48,96]{3,2,1,0:T(8,128)}), f32[3,3,48,96]{3,2,1,0:T(8,128)}) %all-reduce.6.cloned.1.call-update) | async-done | bytes 165904 | tf_op jit(solution)/shard_map/psum | solution.py:119
  126.3 1.6 %broadcast_multiply_fusion = f32[3,3,48,96]{3,2,1,0:T(8,128)} fusion(f32[3,3,48,96]{3,2,1,0:T(8,128)} %all-reduce.6.cloned.1.call-done), kind=kLoop, calls=%fused_computation.138 | loop fusion | flops 41472 | bytes 331776 | tf_op jit(solution)/shard_map/mul | solution.py:123
  128.0 1.0 fusion.57
  129.0 0.4 fusion.40
  129.4 3.7 %all-to-all-start.1 = ((bf16[16,1,48,128]{3,2,1,0:T(8,128)(2,1)}), bf16[16,1,48,128]{3,2,1,0:T(8,128)(2,1)S(1)}, u32[]{:S(2)}, u32[]{:S(2)}) async-start(bf16[16,1,48,128]{3,2,1,0:T(8,128)(2,1)} %fusion.57), calls=%async_computation.1 | async-start | bytes 393216 | tf_op jit(solution)/shard_map/all_to_all | solution.py:39
  133.2 21.3 %psum.15 = f32[9,48]{1,0:T(8,128)S(1)} all-reduce(f32[9,48]{1,0:T(8,128)S(1)} %stack.103), channel_id=1, replica_groups=mesh['groups'=2,'shard'=4,'sub'=2,'chan'=2] {'shard','sub'}, use_global_device_ids=true, to_apply=%region_10.11 | all-reduce | flops 432 | bytes 3456 | tf_op jit(solution)/shard_map/psum | solution.py:119
  154.5 0.6 broadcast_multiply_fusion.1
  155.2 0.7 copy.24
  (29 shorter events, 1.3 us)
Async XLA Ops:
  7.2 15.9 %copy-start = (bf16[3,3,96,96]{3,2,1,0:T(8,128)(2,1)S(1)}, bf16[3,3,96,96]{3,2,1,0:T(8,128)(2,1)}, u32[]{:S(2)}) copy-start(bf16[3,3,96,96]{3,2,1,0:T(8,128)(2,1)} %param.6) | copy-start | bytes 497668
  7.2 13.6 %copy-start.1 = (bf16[4,4,48,128]{3,2,1,0:T(8,128)(2,1)S(1)}, bf16[4,4,48,128]{3,2,1,0:T(8,128)(2,1)}, u32[]{:S(2)}) copy-start(bf16[4,4,48,128]{3,2,1,0:T(8,128)(2,1)} %param.4) | copy-start | bytes 589828
  7.2 13.6 %copy-start.3 = (bf16[9,48]{1,0:T(8,128)(2,1)S(1)}, bf16[9,48]{1,0:T(8,128)(2,1)}, u32[]{:S(2)}) copy-start(bf16[9,48]{1,0:T(8,128)(2,1)} %param.7) | copy-start | bytes 2596
  8.1 12.7 %collective-permute-start = (bf16[4,1,48,128]{3,2,1,0:T(8,128)(2,1)S(1)}, bf16[4,1,48,128]{3,2,1,0:T(8,128)(2,1)S(1)}, u32[]{:S(2)}, u32[]{:S(2)}) collective-permute-start(bf16[4,1,48,128]{3,2,1,0:T(8,128)(2,1)S(1)} %get-tuple-element.24), channel_id=1, source_target_pairs={{0,2},{1,3},{4,6},{5,7},{8,10},{9,11},{12,14},{13,15},{16,18},{17,... | collective-permute-start | bytes 147464 | tf_op jit(solution)/shard_map/ppermute | solution.py:15
  13.0 7.8 %collective-permute-start.1 = (bf16[4,1,48,128]{3,2,1,0:T(8,128)(2,1)S(1)}, bf16[4,1,48,128]{3,2,1,0:T(8,128)(2,1)S(1)}, u32[]{:S(2)}, u32[]{:S(2)}) collective-permute-start(bf16[4,1,48,128]{3,2,1,0:T(8,128)(2,1)S(1)} %get-tuple-element.25), channel_id=1, source_target_pairs={{2,0},{3,1},{6,4},{7,5},{10,8},{11,9},{14,12},{15,13},{18,16},{19,... | collective-permute-start | bytes 147464 | tf_op jit(solution)/shard_map/ppermute | solution.py:17
  15.9 12.2 %all-to-all-start.2 = ((bf16[4,4,48,128]{3,2,0,1:T(8,128)(2,1)}), bf16[4,4,48,128]{3,2,0,1:T(8,128)(2,1)S(1)}, u32[]{:S(2)}, u32[]{:S(2)}) async-start(bf16[4,4,48,128]{3,2,0,1:T(8,128)(2,1)} %copy.19), calls=%async_computation.2 | async-start | bytes 393216 | tf_op jit(solution)/shard_map/all_to_all | solution.py:35
  29.1 9.6 %all-to-all-start.3 = ((bf16[16,1,48,128]{3,2,1,0:T(8,128)(2,1)}), bf16[16,1,48,128]{3,2,1,0:T(8,128)(2,1)S(1)}, u32[]{:S(2)}, u32[]{:S(2)}) async-start(bf16[16,1,48,128]{3,2,1,0:T(8,128)(2,1)} %fusion.56), calls=%async_computation.3 | async-start | bytes 393216 | tf_op jit(solution)/shard_map/all_to_all | solution.py:39
  42.7 85.3 %all-to-all-start = ((bf16[4,4,48,128]{3,2,0,1:T(8,128)(2,1)}), bf16[4,4,48,128]{3,2,0,1:T(8,128)(2,1)S(1)}, u32[]{:S(2)}, u32[]{:S(2)}) async-start(bf16[4,4,48,128]{3,2,0,1:T(8,128)(2,1)} %copy.16), calls=%async_computation | async-start | bytes 393216 | tf_op jit(solution)/shard_map/all_to_all | solution.py:35
  46.1 80.3 %all-reduce.6.cloned.1.call-start = ((), (), s32[]{:S(2)}) async-start(), calls=%async_computation.4 | async-start | bytes 442368 | tf_op jit(solution)/shard_map/psum | solution.py:119
  46.1 6.6 %collective-permute-start.2 = (bf16[4,1,48,128]{3,2,1,0:T(8,128)(2,1)S(1)}, bf16[4,1,48,128]{3,2,1,0:T(8,128)(2,1)S(1)}, u32[]{:S(2)}, u32[]{:S(2)}) collective-permute-start(bf16[4,1,48,128]{3,2,1,0:T(8,128)(2,1)S(1)} %get-tuple-element.22), channel_id=1, source_target_pairs={{0,2},{1,3},{4,6},{5,7},{8,10},{9,11},{12,14},{13,15},{16,18},{17,... | collective-permute-start | bytes 147464 | tf_op jit(solution)/shard_map/ppermute | solution.py:15
  50.7 6.0 %collective-permute-start.3 = (bf16[4,1,48,128]{3,2,1,0:T(8,128)(2,1)S(1)}, bf16[4,1,48,128]{3,2,1,0:T(8,128)(2,1)S(1)}, u32[]{:S(2)}, u32[]{:S(2)}) collective-permute-start(bf16[4,1,48,128]{3,2,1,0:T(8,128)(2,1)S(1)} %get-tuple-element.23), channel_id=1, source_target_pairs={{2,0},{3,1},{6,4},{7,5},{10,8},{11,9},{14,12},{15,13},{18,16},{19,... | collective-permute-start | bytes 147464 | tf_op jit(solution)/shard_map/ppermute | solution.py:17
  56.7 2.4 %copy-start.2 = (bf16[4,4,48,128]{3,2,1,0:T(8,128)(2,1)S(1)}, bf16[4,4,48,128]{3,2,1,0:T(8,128)(2,1)}, u32[]{:S(2)}) copy-start(bf16[4,4,48,128]{3,2,1,0:T(8,128)(2,1)} %param.5) | copy-start | bytes 589828
  129.4 25.8 %all-to-all-start.1 = ((bf16[16,1,48,128]{3,2,1,0:T(8,128)(2,1)}), bf16[16,1,48,128]{3,2,1,0:T(8,128)(2,1)S(1)}, u32[]{:S(2)}, u32[]{:S(2)}) async-start(bf16[16,1,48,128]{3,2,1,0:T(8,128)(2,1)} %fusion.57), calls=%async_computation.1 | async-start | bytes 393216 | tf_op jit(solution)/shard_map/all_to_all | solution.py:39
Sparse Core Ops, SparseCore 0:
  52.9 73.4 all-reduce.5
where the time goes:
time: 163 us
  waiting for transfers between devices  76.4 us (47%)
  starting transfers between devices  27.3 us (17%)
  blocking collectives  25.9 us (16%)
  between operations  14.4 us (9%)
  matrix products  9.13 us (6%)
  other arithmetic  5.67 us (3%)
  local copies, waits for them, and re-layouts  3.97 us (2%)
    psum x1, waiting for transfers between devices, on_device(): lax.psum((space_part, time_part), ('shard', 'sub'))  63.5 us
    psum x1, blocking collectives, on_device(): lax.psum((space_part, time_part), ('shard', 'sub'))  21.3 us
    ppermute x2, starting transfers between devices, with_halo(): lax.ppermute(tail, axis, [(i, (i + 1) % count) for i in range(ends)])  9.39 us
    all_to_all x2, starting transfers between devices, to_time(): lax.all_to_all(values, 'shard', split_axis=1, concat_axis=0, tiled=True)  8.24 us
    all_to_all x2, starting transfers between devices, to_space(): lax.all_to_all(values, 'shard', split_axis=0, concat_axis=1, tiled=True)  7.02 us
    all_to_all x2, waiting for transfers between devices, to_space(): lax.all_to_all(values, 'shard', split_axis=0, concat_axis=1, tiled=True)  5.68 us
    all_gather x2, blocking collectives, widen(): gathered = lax.all_gather(rimmed, 'chan', axis=2, tiled=True)  4.59 us
    ppermute x2, waiting for transfers between devices, with_halo(): lax.ppermute(head, axis, [((i + 1) % count, i) for i in range(ends)])  3.9 us
  transfers between devices with their start and end apart: 9, of which 4 were waited for; matrix products, arithmetic and copies ran while one was open for 7% of the time, Pallas kernels for 0%

commit v1 on v0

--- a/solution.py
+++ b/solution.py
@@ -116,7 +116,7 @@
         space_rows.append(jnp.stack(inner))
     field_grad = back_field.astype(jnp.bfloat16)
     space_part = jnp.stack(space_rows)
-    space_total, time_total = lax.psum((space_part, time_part), ("shard", "sub"))
+    space_total, time_total = lax.psum(lax.psum((space_part, time_part), "sub"), "shard")
     total_frames = frames_here * lax.axis_size("shard")
     total_rows = rows * lax.axis_size("sub")
     scale = float(total_frames * total_rows * cells) ** (-0.5)

time: 163 us -> 126 us (0.77)
  waiting for transfers between devices: 76.4 us -> 43.5 us
  blocking collectives: 25.9 us -> 21.4 us
    psum x1 -> x2, waiting for transfers between devices: 63.5 us -> 30.7 us  [the longest x1 15.4 us: on_device(): lax.psum((space_part, time_part), 'sub')]
    psum x1 -> x2, blocking collectives: 21.3 us -> 16.8 us  [the longest x1 11.8 us: on_device(): lax.psum(lax.psum((space_part, time_part), 'sub'), 'shard')]
  transfers between devices with their start and end apart: 9 -> 10, of which waited for: 4 -> 5; matrix products, arithmetic and copies ran while one was open for 7% -> 10% of each run, Pallas kernels for 0% -> 0%
where the time goes in v1:
time: 126 us; the launch traced here: 125 us
  waiting for transfers between devices  43.5 us (35%)
  starting transfers between devices  27 us (21%)
  blocking collectives  21.4 us (17%)
  between operations  14.5 us (12%)
  matrix products  9.13 us (7%)
  other arithmetic  5.67 us (4%)
  local copies, waits for them, and re-layouts  3.97 us (3%)
    psum x1, waiting for transfers between devices, on_device(): lax.psum((space_part, time_part), 'sub')  15.4 us
    psum x1, waiting for transfers between devices, on_device(): lax.psum(lax.psum((space_part, time_part), 'sub'), 'shard')  15.3 us
    psum x1, blocking collectives, on_device(): lax.psum(lax.psum((space_part, time_part), 'sub'), 'shard')  11.8 us
    ppermute x2, starting transfers between devices, with_halo(): lax.ppermute(tail, axis, [(i, (i + 1) % count) for i in range(ends)])  9.39 us
    all_to_all x2, starting transfers between devices, to_time(): lax.all_to_all(values, 'shard', split_axis=1, concat_axis=0, tiled=True)  8.24 us
    all_to_all x2, starting transfers between devices, to_space(): lax.all_to_all(values, 'shard', split_axis=0, concat_axis=1, tiled=True)  6.74 us
    all_to_all x2, waiting for transfers between devices, to_space(): lax.all_to_all(values, 'shard', split_axis=0, concat_axis=1, tiled=True)  5.68 us
    psum x1, blocking collectives, on_device(): lax.psum((space_part, time_part), 'sub')  5 us
  transfers between devices with their start and end apart: 10, of which 5 were waited for; matrix products, arithmetic and copies ran while one was open for 10% of the time, Pallas kernels for 0%

profile of v1, /device:TPU:0, one launch (start us, length us, event | category | flops | bytes accessed | tf_op | source)
XLA Modules:
  0.0 125.2 jit_solution(15886079160552467753)
XLA Ops:
  7.2 0.9 fusion.95
  8.1 4.9 %collective-permute-start = (bf16[4,1,48,128]{3,2,1,0:T(8,128)(2,1)S(1)}, bf16[4,1,48,128]{3,2,1,0:T(8,128)(2,1)S(1)}, u32[]{:S(2)}, u32[]{:S(2)}) collective-permute-start(bf16[4,1,48,128]{3,2,1,0:T(8,128)(2,1)S(1)} %get-tuple-element.24), channel_id=1, source_target_pairs={{0,2},{1,3},{4,6},{5,7},{8,10},{9,11},{12,14},{13,15},{16,18},{17,... | collective-permute-start | bytes 147464 | tf_op jit(solution)/shard_map/ppermute | solution.py:15
  13.0 1.3 %collective-permute-start.1 = (bf16[4,1,48,128]{3,2,1,0:T(8,128)(2,1)S(1)}, bf16[4,1,48,128]{3,2,1,0:T(8,128)(2,1)S(1)}, u32[]{:S(2)}, u32[]{:S(2)}) collective-permute-start(bf16[4,1,48,128]{3,2,1,0:T(8,128)(2,1)S(1)} %get-tuple-element.25), channel_id=1, source_target_pairs={{2,0},{3,1},{6,4},{7,5},{10,8},{11,9},{14,12},{15,13},{18,16},{19,... | collective-permute-start | bytes 147464 | tf_op jit(solution)/shard_map/ppermute | solution.py:17
  14.3 1.6 %copy.19 = bf16[4,4,48,128]{3,2,0,1:T(8,128)(2,1)} copy(bf16[4,4,48,128]{3,2,1,0:T(8,128)(2,1)} %param.5) | data formatting | bytes 393216 | tf_op args[1]
  15.9 4.9 %all-to-all-start.2 = ((bf16[4,4,48,128]{3,2,0,1:T(8,128)(2,1)}), bf16[4,4,48,128]{3,2,0,1:T(8,128)(2,1)S(1)}, u32[]{:S(2)}, u32[]{:S(2)}) async-start(bf16[4,4,48,128]{3,2,0,1:T(8,128)(2,1)} %copy.19), calls=%async_computation.2 | async-start | bytes 393216 | tf_op jit(solution)/shard_map/all_to_all | solution.py:35
  20.9 2.2 %all_gather.6 = bf16[4,6,96,128]{3,2,1,0:T(8,128)(2,1)S(1)} all-gather(bf16[4,6,48,128]{3,2,1,0:T(8,128)(2,1)S(1)} %pad_maximum_fusion), channel_id=1, replica_groups=mesh['groups'=2,'shard'=4,'sub'=2,'chan'=2] {'chan'}, dimensions={2}, use_global_device_ids=true | all-gather | bytes 884736 | tf_op jit(solution)/shard_map/all_gather | solution.py:30
  23.1 0.3 fusion.55
  23.6 0.3 convolution_add_fusion.6
  23.9 0.3 convolution_add_fusion.5
  24.5 0.3 convolution_add_fusion.3
  24.8 3.2 %all-to-all-done.2 = bf16[4,4,48,128]{3,2,0,1:T(8,128)(2,1)S(1)} async-done(((bf16[4,4,48,128]{3,2,0,1:T(8,128)(2,1)}), bf16[4,4,48,128]{3,2,0,1:T(8,128)(2,1)S(1)}, u32[]{:S(2)}, u32[]{:S(2)}) %all-to-all-start.2) | async-done | bytes 196640 | tf_op jit(solution)/shard_map/all_to_all | solution.py:35
  28.1 1.0 fusion.56
  29.1 3.4 %all-to-all-start.3 = ((bf16[16,1,48,128]{3,2,1,0:T(8,128)(2,1)}), bf16[16,1,48,128]{3,2,1,0:T(8,128)(2,1)S(1)}, u32[]{:S(2)}, u32[]{:S(2)}) async-start(bf16[16,1,48,128]{3,2,1,0:T(8,128)(2,1)} %fusion.56), calls=%async_computation.3 | async-start | bytes 393216 | tf_op jit(solution)/shard_map/all_to_all | solution.py:39
  32.4 0.3 convolution_add_fusion.2
  33.0 5.7 %all-to-all-done.3 = bf16[16,1,48,128]{3,2,1,0:T(8,128)(2,1)S(1)} async-done(((bf16[16,1,48,128]{3,2,1,0:T(8,128)(2,1)}), bf16[16,1,48,128]{3,2,1,0:T(8,128)(2,1)S(1)}, u32[]{:S(2)}, u32[]{:S(2)}) %all-to-all-start.3) | async-done | bytes 196640 | tf_op jit(solution)/shard_map/all_to_all | solution.py:39
  38.7 0.6 fusion.26
  39.5 0.3 convolution_bitcast_fusion.11
  39.8 0.3 convolution_bitcast_fusion.12
  40.4 0.3 convolution_bitcast_fusion.14
  40.7 0.3 convolution_bitcast_fusion.15
  41.3 0.3 convolution_bitcast_fusion.17
  41.7 0.3 convolution_bitcast_fusion.9
  42.0 0.7 copy.16
  42.7 3.4 %all-to-all-start = ((bf16[4,4,48,128]{3,2,0,1:T(8,128)(2,1)}), bf16[4,4,48,128]{3,2,0,1:T(8,128)(2,1)S(1)}, u32[]{:S(2)}, u32[]{:S(2)}) async-start(bf16[4,4,48,128]{3,2,0,1:T(8,128)(2,1)} %copy.16), calls=%async_computation | async-start | bytes 393216 | tf_op jit(solution)/shard_map/all_to_all | solution.py:35
  46.1 4.5 %collective-permute-start.2 = (bf16[4,1,48,128]{3,2,1,0:T(8,128)(2,1)S(1)}, bf16[4,1,48,128]{3,2,1,0:T(8,128)(2,1)S(1)}, u32[]{:S(2)}, u32[]{:S(2)}) collective-permute-start(bf16[4,1,48,128]{3,2,1,0:T(8,128)(2,1)S(1)} %get-tuple-element.22), channel_id=1, source_target_pairs={{0,2},{1,3},{4,6},{5,7},{8,10},{9,11},{12,14},{13,15},{16,18},{17,... | collective-permute-start | bytes 147464 | tf_op jit(solution)/shard_map/ppermute | solution.py:15
  50.7 1.3 %collective-permute-start.3 = (bf16[4,1,48,128]{3,2,1,0:T(8,128)(2,1)S(1)}, bf16[4,1,48,128]{3,2,1,0:T(8,128)(2,1)S(1)}, u32[]{:S(2)}, u32[]{:S(2)}) collective-permute-start(bf16[4,1,48,128]{3,2,1,0:T(8,128)(2,1)S(1)} %get-tuple-element.23), channel_id=1, source_target_pairs={{2,0},{3,1},{6,4},{7,5},{10,8},{11,9},{14,12},{15,13},{18,16},{19,... | collective-permute-start | bytes 147464 | tf_op jit(solution)/shard_map/ppermute | solution.py:17
  52.0 0.7 pad_maximum_fusion.2
  52.8 3.9 %collective-permute-done.3 = bf16[4,1,48,128]{3,2,1,0:T(8,128)(2,1)S(1)} collective-permute-done((bf16[4,1,48,128]{3,2,1,0:T(8,128)(2,1)S(1)}, bf16[4,1,48,128]{3,2,1,0:T(8,128)(2,1)S(1)}, u32[]{:S(2)}, u32[]{:S(2)}) %collective-permute-start.3) | collective-permute-done | bytes 49184 | tf_op jit(solution)/shard_map/ppermute | solution.py:17
  56.7 2.4 %all_gather.7 = bf16[4,6,96,128]{3,2,1,0:T(8,128)(2,1)S(1)} all-gather(bf16[4,6,48,128]{3,2,1,0:T(8,128)(2,1)S(1)} %pad_maximum_fusion.1), channel_id=1, replica_groups=mesh['groups'=2,'shard'=4,'sub'=2,'chan'=2] {'chan'}, dimensions={2}, use_global_device_ids=true | all-gather | bytes 884736 | tf_op jit(solution)/shard_map/all_gather | solution.py:30
  59.1 0.3 fusion.8
  59.4 0.3 fusion.7
  59.7 0.3 fusion.6
  60.1 0.3 fusion.5
  60.4 0.3 fusion.4
  60.8 0.3 fusion.3
  61.1 0.3 fusion.2
  61.5 0.3 fusion.1
  61.8 1.0 fusion.10
  62.8 15.4 %all-reduce.7.cloned.1.call-done = f32[3,3,48,96]{3,2,1,0:T(8,128)} async-done(((f32[3,3,48,96]{3,2,1,0:T(8,128)}), f32[3,3,48,96]{3,2,1,0:T(8,128)}) %all-reduce.7.cloned.1.call-update) | async-done | bytes 165904 | tf_op jit(solution)/shard_map/psum | solution.py:119
  78.2 1.0 fusion.57
  79.3 0.4 fusion.40
  79.8 5.0 %psum.30 = f32[9,48]{1,0:T(8,128)S(1)} all-reduce(f32[9,48]{1,0:T(8,128)S(1)} %stack.103), channel_id=1, replica_groups=mesh['groups'=2,'shard'=4,'sub'=2,'chan'=2] {'sub'}, use_global_device_ids=true, to_apply=%region_11.12 | all-reduce | flops 432 | bytes 3456 | tf_op jit(solution)/shard_map/psum | solution.py:119
  84.8 11.8 %psum.31 = f32[9,48]{1,0:T(8,128)S(1)} all-reduce(f32[9,48]{1,0:T(8,128)S(1)} %psum.30), channel_id=1, replica_groups=mesh['groups'=2,'shard'=4,'sub'=2,'chan'=2] {'shard'}, use_global_device_ids=true, to_apply=%region_12.13 | all-reduce | flops 432 | bytes 3456 | tf_op jit(solution)/shard_map/psum | solution.py:119
  96.7 3.4 %all-to-all-start.1 = ((bf16[16,1,48,128]{3,2,1,0:T(8,128)(2,1)}), bf16[16,1,48,128]{3,2,1,0:T(8,128)(2,1)S(1)}, u32[]{:S(2)}, u32[]{:S(2)}) async-start(bf16[16,1,48,128]{3,2,1,0:T(8,128)(2,1)} %fusion.57), calls=%async_computation.1 | async-start | bytes 393216 | tf_op jit(solution)/shard_map/all_to_all | solution.py:39
  100.1 0.6 broadcast_multiply_fusion.1
  100.7 15.3 %all-reduce.9.cloned.1.call-done = f32[3,3,48,96]{3,2,1,0:T(8,128)} async-done(((f32[3,3,48,96]{3,2,1,0:T(8,128)}), f32[3,3,48,96]{3,2,1,0:T(8,128)}) %all-reduce.9.cloned.1.call-update) | async-done | bytes 165904 | tf_op jit(solution)/shard_map/psum | solution.py:119
  116.0 1.6 %broadcast_multiply_fusion = f32[3,3,48,96]{3,2,1,0:T(8,128)} fusion(f32[3,3,48,96]{3,2,1,0:T(8,128)} %all-reduce.9.cloned.1.call-done), kind=kLoop, calls=%fused_computation.138 | loop fusion | flops 41472 | bytes 331776 | tf_op jit(solution)/shard_map/mul | solution.py:123
  117.7 0.7 copy.24
  (33 shorter events, 1.8 us)
Async XLA Ops:
  7.2 15.9 %copy-start = (bf16[3,3,96,96]{3,2,1,0:T(8,128)(2,1)S(1)}, bf16[3,3,96,96]{3,2,1,0:T(8,128)(2,1)}, u32[]{:S(2)}) copy-start(bf16[3,3,96,96]{3,2,1,0:T(8,128)(2,1)} %param.6) | copy-start | bytes 497668
  7.2 13.6 %copy-start.1 = (bf16[4,4,48,128]{3,2,1,0:T(8,128)(2,1)S(1)}, bf16[4,4,48,128]{3,2,1,0:T(8,128)(2,1)}, u32[]{:S(2)}) copy-start(bf16[4,4,48,128]{3,2,1,0:T(8,128)(2,1)} %param.4) | copy-start | bytes 589828
  7.2 13.6 %copy-start.3 = (bf16[9,48]{1,0:T(8,128)(2,1)S(1)}, bf16[9,48]{1,0:T(8,128)(2,1)}, u32[]{:S(2)}) copy-start(bf16[9,48]{1,0:T(8,128)(2,1)} %param.7) | copy-start | bytes 2596
  8.1 12.7 %collective-permute-start = (bf16[4,1,48,128]{3,2,1,0:T(8,128)(2,1)S(1)}, bf16[4,1,48,128]{3,2,1,0:T(8,128)(2,1)S(1)}, u32[]{:S(2)}, u32[]{:S(2)}) collective-permute-start(bf16[4,1,48,128]{3,2,1,0:T(8,128)(2,1)S(1)} %get-tuple-element.24), channel_id=1, source_target_pairs={{0,2},{1,3},{4,6},{5,7},{8,10},{9,11},{12,14},{13,15},{16,18},{17,... | collective-permute-start | bytes 147464 | tf_op jit(solution)/shard_map/ppermute | solution.py:15
  13.0 7.8 %collective-permute-start.1 = (bf16[4,1,48,128]{3,2,1,0:T(8,128)(2,1)S(1)}, bf16[4,1,48,128]{3,2,1,0:T(8,128)(2,1)S(1)}, u32[]{:S(2)}, u32[]{:S(2)}) collective-permute-start(bf16[4,1,48,128]{3,2,1,0:T(8,128)(2,1)S(1)} %get-tuple-element.25), channel_id=1, source_target_pairs={{2,0},{3,1},{6,4},{7,5},{10,8},{11,9},{14,12},{15,13},{18,16},{19,... | collective-permute-start | bytes 147464 | tf_op jit(solution)/shard_map/ppermute | solution.py:17
  15.9 12.2 %all-to-all-start.2 = ((bf16[4,4,48,128]{3,2,0,1:T(8,128)(2,1)}), bf16[4,4,48,128]{3,2,0,1:T(8,128)(2,1)S(1)}, u32[]{:S(2)}, u32[]{:S(2)}) async-start(bf16[4,4,48,128]{3,2,0,1:T(8,128)(2,1)} %copy.19), calls=%async_computation.2 | async-start | bytes 393216 | tf_op jit(solution)/shard_map/all_to_all | solution.py:35
  29.1 9.6 %all-to-all-start.3 = ((bf16[16,1,48,128]{3,2,1,0:T(8,128)(2,1)}), bf16[16,1,48,128]{3,2,1,0:T(8,128)(2,1)S(1)}, u32[]{:S(2)}, u32[]{:S(2)}) async-start(bf16[16,1,48,128]{3,2,1,0:T(8,128)(2,1)} %fusion.56), calls=%async_computation.3 | async-start | bytes 393216 | tf_op jit(solution)/shard_map/all_to_all | solution.py:39
  42.7 35.5 %all-to-all-start = ((bf16[4,4,48,128]{3,2,0,1:T(8,128)(2,1)}), bf16[4,4,48,128]{3,2,0,1:T(8,128)(2,1)S(1)}, u32[]{:S(2)}, u32[]{:S(2)}) async-start(bf16[4,4,48,128]{3,2,0,1:T(8,128)(2,1)} %copy.16), calls=%async_computation | async-start | bytes 393216 | tf_op jit(solution)/shard_map/all_to_all | solution.py:35
  46.1 32.1 %all-reduce.7.cloned.1.call-start = ((), (), s32[]{:S(2)}) async-start(), calls=%async_computation.4 | async-start | bytes 442368 | tf_op jit(solution)/shard_map/psum | solution.py:119
  46.1 6.7 %collective-permute-start.2 = (bf16[4,1,48,128]{3,2,1,0:T(8,128)(2,1)S(1)}, bf16[4,1,48,128]{3,2,1,0:T(8,128)(2,1)S(1)}, u32[]{:S(2)}, u32[]{:S(2)}) collective-permute-start(bf16[4,1,48,128]{3,2,1,0:T(8,128)(2,1)S(1)} %get-tuple-element.22), channel_id=1, source_target_pairs={{0,2},{1,3},{4,6},{5,7},{8,10},{9,11},{12,14},{13,15},{16,18},{17,... | collective-permute-start | bytes 147464 | tf_op jit(solution)/shard_map/ppermute | solution.py:15
  50.7 6.0 %collective-permute-start.3 = (bf16[4,1,48,128]{3,2,1,0:T(8,128)(2,1)S(1)}, bf16[4,1,48,128]{3,2,1,0:T(8,128)(2,1)S(1)}, u32[]{:S(2)}, u32[]{:S(2)}) collective-permute-start(bf16[4,1,48,128]{3,2,1,0:T(8,128)(2,1)S(1)} %get-tuple-element.23), channel_id=1, source_target_pairs={{2,0},{3,1},{6,4},{7,5},{10,8},{11,9},{14,12},{15,13},{18,16},{19,... | collective-permute-start | bytes 147464 | tf_op jit(solution)/shard_map/ppermute | solution.py:17
  52.7 63.2 %all-reduce.9.cloned.1.call-start = ((), (), s32[]{:S(2)}) async-start(), calls=%async_computation.5 | async-start | bytes 442368 | tf_op jit(solution)/shard_map/psum | solution.py:119
  56.7 2.4 %copy-start.2 = (bf16[4,4,48,128]{3,2,1,0:T(8,128)(2,1)S(1)}, bf16[4,4,48,128]{3,2,1,0:T(8,128)(2,1)}, u32[]{:S(2)}) copy-start(bf16[4,4,48,128]{3,2,1,0:T(8,128)(2,1)} %param.5) | copy-start | bytes 589828
  96.7 20.9 %all-to-all-start.1 = ((bf16[16,1,48,128]{3,2,1,0:T(8,128)(2,1)}), bf16[16,1,48,128]{3,2,1,0:T(8,128)(2,1)S(1)}, u32[]{:S(2)}, u32[]{:S(2)}) async-start(bf16[16,1,48,128]{3,2,1,0:T(8,128)(2,1)} %fusion.57), calls=%async_computation.1 | async-start | bytes 393216 | tf_op jit(solution)/shard_map/all_to_all | solution.py:39
Sparse Core Ops, SparseCore 0:
  52.9 25.2 all-reduce.6
  80.5 35.3 all-reduce.8
